TPU v7x, 32 devices: a whole 2x2x4 slice. The times are simulated.
32 devices in a mesh: gz: 8 (over z, core), grp: 4 (over y, x).
Axes of the slice: x: 2, y: 2, z: 4, core: 2. Of those that a mesh axis runs over, the one named last changes fastest.
Arguments:
- volumes: bfloat16 [4, 16, 16, 1024], P('grp', 'gz'), may hold values from -6 to 6
- cotangent: bfloat16 [4, 8, 64, 128], P(None, 'gz', None, 'grp'), may hold values from -6 to 6
- fine_kernel: bfloat16 [1728, 64], replicated, may hold values from -0.15625 to 0.15625
- down_kernel: bfloat16 [512, 128], replicated, may hold values from -0.25 to 0.25
- coarse_kernel: bfloat16 [3456, 128], P(None, 'grp'), may hold values from -0.109375 to 0.109375
Outputs:
- coarse_out: bfloat16 [4, 8, 64, 128], P(None, 'gz', None, 'grp')
- volume_grad: bfloat16 [4, 16, 16, 1024], P('grp', 'gz')
- fine_kernel_grad: float32 [1728, 64], replicated
- down_kernel_grad: float32 [512, 128], replicated
- coarse_kernel_grad: float32 [3456, 128], P(None, 'grp')
All inputs are finite; a program needn't handle non-finite values.
Results may differ from a plain program's by a relative error of at most 0.019.
Values may be sent and summed in bfloat16 or wider, within the bound.
A program may use at most 64 MiB of HBM per device.

v0:
```python
import jax
import jax.numpy as jnp
from jax import lax
from jax.sharding import PartitionSpec as P


def with_halo(array, sides, width):
    for axis, dim in sides:
        devices, length = (lax.axis_size(axis), array.shape[dim])
        up = [(i, (i + 1) % devices) for i in range(devices - 1)]
        down = [(j, i) for i, j in up]
        last = lax.slice_in_dim(array, length - width, length, axis=dim)
        initial = lax.slice_in_dim(array, 0, width, axis=dim)
        before = lax.ppermute(last, axis, up)
        after = lax.ppermute(initial, axis, down)
        array = jnp.concatenate([before, array, after], axis=dim)
    return array


def pad_sides(block):
    return jnp.pad(block, ((0, 0), (0, 0), (1, 1), (1, 1), (0, 0)))


def convolve(padded, kernel):
    samples, extent_z, extent_x, extent_y, channels = padded.shape
    extent_z, extent_x, extent_y = (extent_z - 2, extent_x - 2, extent_y - 2)
    summed = None
    for plane in range(3):
        pieces = [
            padded[
                :,
                plane : plane + extent_z,
                row_step : row_step + extent_x,
                col_step : col_step + extent_y,
                :,
            ]
            for row_step in range(3)
            for col_step in range(3)
        ]
        columns = jnp.concatenate(pieces, axis=-1).reshape(-1, 9 * channels)
        rows = kernel[plane * 9 * channels : (plane + 1) * 9 * channels]
        partial_value = jnp.dot(columns, rows, preferred_element_type=jnp.float32)
        summed = partial_value if summed is None else summed + partial_value
    return summed.reshape(samples, extent_z, extent_x, extent_y, -1)


def kernel_gradient(padded, grad):
    samples, extent_z, extent_x, extent_y, channels = padded.shape
    extent_z, extent_x, extent_y = (extent_z - 2, extent_x - 2, extent_y - 2)
    flat_grad = grad.reshape(-1, grad.shape[-1])
    blocks = []
    for plane in range(3):
        pieces = [
            padded[
                :,
                plane : plane + extent_z,
                row_step : row_step + extent_x,
                col_step : col_step + extent_y,
                :,
            ]
            for row_step in range(3)
            for col_step in range(3)
        ]
        columns = jnp.concatenate(pieces, axis=-1).reshape(-1, 9 * channels)
        blocks.append(
            lax.dot_general(
                columns, flat_grad, (((0,), (0,)), ((), ())), preferred_element_type=jnp.float32
            )
        )
    return jnp.concatenate(blocks, axis=0)


def flip_kernel(kernel, inputs):
    outputs = kernel.shape[1]
    shaped = kernel.reshape(3, 3, 3, inputs, outputs)[::-1, ::-1, ::-1]
    return jnp.transpose(shaped, (0, 1, 2, 4, 3)).reshape(27 * outputs, inputs)


def silu_slope(value):
    sigmoid_v = jax.nn.sigmoid(value)
    return sigmoid_v * (1.0 + value * (1.0 - sigmoid_v))


def pool_columns(block):
    samples, extent_z, extent_x, extent_y, channels = block.shape
    shaped = block.reshape(samples, extent_z // 2, 2, extent_x // 2, 2, extent_y // 2, 2, channels)
    return jnp.transpose(shaped, (0, 1, 3, 5, 2, 4, 6, 7)).reshape(-1, 8 * channels)


def unpool_columns(flat, samples, extent_z, extent_x, extent_y, channels):
    shaped = flat.reshape(samples, extent_z // 2, extent_x // 2, extent_y // 2, 2, 2, 2, channels)
    return jnp.transpose(shaped, (0, 1, 4, 2, 5, 3, 6, 7)).reshape(
        samples, extent_z, extent_x, extent_y, channels
    )


def coarse_rim(block):
    return with_halo(block, (("gz", 1),), 1)


def coarse_grad_rim(block):
    return with_halo(block, (("gz", 1),), 1)


def coarse_kernel_total(partial_value):
    return lax.psum(partial_value.astype(jnp.bfloat16), "gz").astype(jnp.float32)


def per_device(volumes, cotangent, fine_kernel, down_kernel, coarse_kernel):
    samples, planes, xfine, packed = volumes.shape
    cfine = fine_kernel.shape[1]
    yfine = packed // cfine
    fine = volumes.reshape(samples, planes, xfine, yfine, cfine)
    fine_padded = pad_sides(with_halo(fine, (("gz", 1),), 1))
    fine_pre = convolve(fine_padded, fine_kernel)
    fine_act = jax.nn.silu(fine_pre).astype(jnp.bfloat16)
    pooled = pool_columns(fine_act)
    coarse_in = jnp.dot(pooled, down_kernel, preferred_element_type=jnp.float32).astype(
        jnp.bfloat16
    )
    coarse_in = coarse_in.reshape(samples, planes // 2, xfine // 2, yfine // 2, -1)
    coarse_framed = coarse_rim(coarse_in)
    gathered = pad_sides(lax.all_gather(coarse_framed, "grp", axis=0, tiled=True))
    coarse_pre = convolve(gathered, coarse_kernel)
    group, zcoarse, xcoarse, ycoarse, own_channels = coarse_pre.shape
    coarse_out = (
        jax.nn.silu(coarse_pre)
        .astype(jnp.bfloat16)
        .reshape(group, zcoarse, xcoarse * ycoarse, own_channels)
    )
    grad_shaped = cotangent.reshape(coarse_pre.shape).astype(jnp.float32)
    coarse_grad = (grad_shaped * silu_slope(coarse_pre)).astype(jnp.bfloat16)
    coarse_kg = coarse_kernel_total(kernel_gradient(gathered, coarse_grad))
    partial_value = convolve(
        pad_sides(coarse_grad_rim(coarse_grad)),
        flip_kernel(coarse_kernel, coarse_kernel.shape[0] // 27),
    )
    coarse_in_grad = lax.psum_scatter(
        partial_value.astype(jnp.bfloat16), "grp", scatter_dimension=0, tiled=True
    )
    flat_in_grad = coarse_in_grad.reshape(-1, coarse_in_grad.shape[-1])
    pooled_grad = jnp.dot(flat_in_grad, down_kernel.T, preferred_element_type=jnp.float32)
    fine_act_grad = unpool_columns(pooled_grad, samples, planes, xfine, yfine, cfine)
    down_kg = lax.dot_general(
        pooled, flat_in_grad, (((0,), (0,)), ((), ())), preferred_element_type=jnp.float32
    )
    fine_grad = (fine_act_grad * silu_slope(fine_pre)).astype(jnp.bfloat16)
    fine_kg = kernel_gradient(fine_padded, fine_grad)
    fine_kg, down_kg = lax.psum((fine_kg, down_kg), ("gz", "grp"))
    grad_padded = pad_sides(with_halo(fine_grad, (("gz", 1),), 1))
    volume_grad = convolve(grad_padded, flip_kernel(fine_kernel, cfine)).astype(jnp.bfloat16)
    volume_grad = volume_grad.reshape(samples, planes, xfine, packed)
    return (coarse_out, volume_grad, fine_kg, down_kg, coarse_kg)


def solution(mesh):
    in_specs = (P("grp", "gz", None, None), P(None, "gz", None, "grp"), P(), P(), P(None, "grp"))
    out_specs = (P(None, "gz", None, "grp"), P("grp", "gz", None, None), P(), P(), P(None, "grp"))
    return jax.shard_map(
        per_device, mesh=mesh, in_specs=in_specs, out_specs=out_specs, check_vma=False
    )
```

profile of v0, /device:TPU:0, one launch (start us, length us, event | category | flops | bytes accessed | tf_op | source)
XLA Modules:
  0.0 269.8 jit_solution(286053441385954328)
XLA Ops:
  8.1 1.1 reshape.446
  9.2 2.5 collective-permute-start
  11.7 1.3 collective-permute-start.1
  13.2 0.7 rev.6
  13.9 3.1 %collective-permute-done.1 = bf16[1,1,16,16,64]{4,3,2,1,0:T(8,128)(2,1)S(1)} collective-permute-done((bf16[1,1,16,16,64]{4,3,2,1,0:T(8,128)(2,1)S(1)}, bf16[1,1,16,16,64]{4,3,2,1,0:T(8,128)(2,1)S(1)}, u32[]{:S(2)}, u32[]{:S(2)}) %collective-permute-start.1) | collective-permute-done | bytes 32800 | tf_op jit(solution)/shard_map/ppermute | solution.py:15
  17.2 1.2 fusion.44
  19.7 1.0 fusion.26
  20.8 0.8 copy-done.36
  22.3 1.3 convolution_add_fusion.3
  25.4 0.5 copy-done.1
  26.6 4.8 %collective-permute-start.2 = (bf16[1,1,8,8,128]{4,3,2,0,1:T(8,128)(2,1)S(1)}, bf16[1,1,8,8,128]{4,3,2,0,1:T(8,128)(2,1)S(1)}, u32[]{:S(2)}, u32[]{:S(2)}) collective-permute-start(bf16[1,1,8,8,128]{4,3,2,0,1:T(8,128)(2,1)S(1)} %fusion.6), channel_id=1, source_target_pairs={{0,4},{4,8},{8,12},{12,16},{16,20},{20,24},{24,28},{1,5},{5,9},{9,... | collective-permute-start | bytes 49160 | tf_op jit(solution)/shard_map/ppermute | solution.py:14
  31.5 1.3 collective-permute-start.3
  32.9 0.6 copy-done.43
  33.5 0.7 copy.163
  34.6 0.7 reshape.475
  35.3 0.6 copy.175
  36.0 0.6 copy.176
  36.6 0.6 copy.165
  37.3 2.9 %rev.7 = bf16[3,3,3,64,64]{3,2,1,0,4:T(4,128)(2,1)} reverse(bf16[3,3,3,64,64]{3,2,1,0,4:T(4,128)(2,1)S(1)} %reshape.464), dimensions={0,1,2} | reverse | bytes 442368 | tf_op jit(solution)/shard_map/rev | solution.py:75
  40.2 8.8 %all_gather.3 = bf16[4,3,8,8,128]{4,3,2,0,1:T(8,128)(2,1)S(1)} all-gather(bf16[1,3,8,8,128]{4,3,2,0,1:T(8,128)(2,1)S(1)} %pad_maximum_fusion.5), channel_id=1, replica_groups=mesh['gz'=8,'grp'=4] {'grp'}, dimensions={0}, use_global_device_ids=true | all-gather | bytes 245760 | tf_op jit(solution)/shard_map/all_gather | solution.py:123
  49.9 0.9 copy-done.22
  51.6 0.8 reshape.455
  52.4 1.5 multiply_convert_fusion.4
  53.9 0.9 copy.197
  54.7 0.9 fusion
  56.1 0.5 copy-done.40
  56.7 0.8 copy-done.41
  57.6 1.3 collective-permute-start.4
  58.9 1.3 collective-permute-start.5
  60.2 0.7 pad_maximum_fusion
  61.0 3.4 %collective-permute-done.5 = bf16[4,1,8,8,32]{4,3,2,0,1:T(8,128)(2,1)S(1)} collective-permute-done((bf16[4,1,8,8,32]{4,3,2,0,1:T(8,128)(2,1)S(1)}, bf16[4,1,8,8,32]{4,3,2,0,1:T(8,128)(2,1)S(1)}, u32[]{:S(2)}, u32[]{:S(2)}) %collective-permute-start.5) | collective-permute-done | bytes 16416 | tf_op jit(solution)/shard_map/ppermute | solution.py:15
  65.0 0.6 constant_dynamic-update-slice_fusion.35
  66.2 0.7 copy-done.57
  66.9 0.7 copy-done.58
  67.7 0.8 copy-done.46
  69.1 0.6 copy-done.45
  70.2 0.6 copy-done.42
  70.8 0.8 fusion.4
  71.9 0.7 copy.191
  72.6 0.7 copy.180
  73.3 0.7 copy.192
  74.9 43.0 %all-reduce.9.cloned.1.call-done = bf16[3456,32]{0,1:T(8,128)(2,1)} async-done(((bf16[3456,32]{0,1:T(8,128)(2,1)}), bf16[3456,32]{0,1:T(8,128)(2,1)}) %all-reduce.9.cloned.1.call-update) | async-done | bytes 221200 | tf_op jit(solution)/shard_map/psum | solution.py:106
  117.8 1.7 convert_element_type.157
  119.6 1.0 multiply_convert_fusion
  121.5 1.9 collective-permute-start.6
  123.4 1.5 collective-permute-start.7
  124.9 0.9 fusion.37
  126.2 0.9 concatenate.174
  127.2 2.1 collective-permute-done.7
  129.9 1.1 fusion.42
  131.3 1.6 copy.184
  132.9 1.6 copy.185
  134.5 1.6 copy.186
  136.1 1.6 copy.187
  138.0 0.7 copy-done.50
  138.8 0.8 copy-done.51
  139.6 0.9 copy-done.19
  140.6 0.8 copy-done.48
  141.4 0.9 copy-done.27
  142.6 0.6 copy-done.54
  145.8 0.8 convert_element_type.151
  146.6 113.2 %all-reduce.11.cloned.1.call-done = (f32[1728,64]{0,1:T(8,128)}, f32[512,128]{1,0:T(8,128)}) async-done(((f32[1728,64]{0,1:T(8,128)}, f32[512,128]{1,0:T(8,128)}), (f32[1728,64]{0,1:T(8,128)}, f32[512,128]{1,0:T(8,128)})) %all-reduce.11.cloned.1.call-update) | async-done | bytes 704528 | tf_op jit(solution)/shard_map/psum | solution.py:149
  259.8 1.9 copy.254
  261.7 0.7 copy.255
  (218 shorter events, 16.1 us)
Async XLA Ops:
  8.0 18.0 %copy-start = (bf16[512,128]{1,0:T(8,128)(2,1)S(1)}, bf16[512,128]{1,0:T(8,128)(2,1)}, u32[]{:S(2)}) copy-start(bf16[512,128]{1,0:T(8,128)(2,1)} %param.8) | copy-start | bytes 393220
  8.0 109.8 %all-reduce.9.cloned.1.call-start = ((), (), s32[]{:S(2)}) async-start(), calls=%async_computation.1 | async-start | bytes 442368 | tf_op jit(solution)/shard_map/psum | solution.py:106
  8.1 5.0 %copy-start.47 = (bf16[1,2,16,1024]{3,2,1,0:T(8,128)(2,1)S(1)}, bf16[1,2,16,1024]{3,2,1,0:T(8,128)(2,1)}, u32[]{:S(2)}) copy-start(bf16[1,2,16,1024]{3,2,1,0:T(8,128)(2,1)} %param.5) | copy-start | bytes 196612
  9.1 4.0 %copy-start.21 = (bf16[3456,32]{0,1:T(8,128)(2,1)S(1)}, bf16[3456,32]{0,1:T(8,128)(2,1)}, u32[]{:S(2)}) copy-start(bf16[3456,32]{0,1:T(8,128)(2,1)} %param.9) | copy-start | bytes 663556
  9.2 4.8 %collective-permute-start = (bf16[1,1,16,16,64]{4,3,2,1,0:T(8,128)(2,1)S(1)}, bf16[1,1,16,16,64]{4,3,2,1,0:T(8,128)(2,1)S(1)}, u32[]{:S(2)}, u32[]{:S(2)}) collective-permute-start(bf16[1,1,16,16,64]{4,3,2,1,0:T(8,128)(2,1)S(1)} %get-tuple-element.108), channel_id=1, source_target_pairs={{0,4},{4,8},{8,12},{12,16},{16,20},{20,24},{24,28},{1,5},{5,9},{9,... | collective-permute-start | bytes 98312 | tf_op jit(solution)/shard_map/ppermute | solution.py:14
  11.7 5.3 %collective-permute-start.1 = (bf16[1,1,16,16,64]{4,3,2,1,0:T(8,128)(2,1)S(1)}, bf16[1,1,16,16,64]{4,3,2,1,0:T(8,128)(2,1)S(1)}, u32[]{:S(2)}, u32[]{:S(2)}) collective-permute-start(bf16[1,1,16,16,64]{4,3,2,1,0:T(8,128)(2,1)S(1)} %get-tuple-element.109), channel_id=1, source_target_pairs={{4,0},{8,4},{12,8},{16,12},{20,16},{24,20},{28,24},{5,1},{9,5},{13... | collective-permute-start | bytes 98312 | tf_op jit(solution)/shard_map/ppermute | solution.py:15
  18.5 0.8 copy-start.10
  18.5 0.8 copy-start.12
  18.5 0.9 copy-start.14
  18.5 0.9 copy-start.16
  18.5 1.2 copy-start.20
  20.7 0.9 copy-start.36
  20.7 1.0 copy-start.37
  20.7 1.0 copy-start.38
  21.7 1.9 copy-start.35
  22.2 1.4 copy-start.28
  22.2 1.4 copy-start.29
  22.2 1.4 copy-start.30
  22.2 1.4 copy-start.31
  22.3 1.4 copy-start.32
  22.3 1.4 copy-start.33
  22.3 1.4 copy-start.34
  26.6 13.5 %collective-permute-start.2 = (bf16[1,1,8,8,128]{4,3,2,0,1:T(8,128)(2,1)S(1)}, bf16[1,1,8,8,128]{4,3,2,0,1:T(8,128)(2,1)S(1)}, u32[]{:S(2)}, u32[]{:S(2)}) collective-permute-start(bf16[1,1,8,8,128]{4,3,2,0,1:T(8,128)(2,1)S(1)} %fusion.6), channel_id=1, source_target_pairs={{0,4},{4,8},{8,12},{12,16},{16,20},{20,24},{24,28},{1,5},{5,9},{9,... | collective-permute-start | bytes 49160 | tf_op jit(solution)/shard_map/ppermute | solution.py:14
  31.5 8.7 %collective-permute-start.3 = (bf16[1,1,8,8,128]{4,3,2,0,1:T(8,128)(2,1)S(1)}, bf16[1,1,8,8,128]{4,3,2,0,1:T(8,128)(2,1)S(1)}, u32[]{:S(2)}, u32[]{:S(2)}) collective-permute-start(bf16[1,1,8,8,128]{4,3,2,0,1:T(8,128)(2,1)S(1)} %fusion.6), channel_id=1, source_target_pairs={{4,0},{8,4},{12,8},{16,12},{20,16},{24,20},{28,24},{5,1},{9,5},{13... | collective-permute-start | bytes 49160 | tf_op jit(solution)/shard_map/ppermute | solution.py:15
  32.8 0.8 copy-start.43
  49.8 0.9 copy-start.22
  51.6 0.8 copy-start.39
  55.9 0.8 copy-start.40
  56.6 0.9 copy-start.41
  57.5 2.7 copy-start.44
  57.6 3.4 %collective-permute-start.4 = (bf16[4,1,8,8,32]{4,3,2,0,1:T(8,128)(2,1)S(1)}, bf16[4,1,8,8,32]{4,3,2,0,1:T(8,128)(2,1)S(1)}, u32[]{:S(2)}, u32[]{:S(2)}) collective-permute-start(bf16[4,1,8,8,32]{4,3,2,0,1:T(8,128)(2,1)S(1)} %fusion.23), channel_id=1, source_target_pairs={{0,4},{4,8},{8,12},{12,16},{16,20},{20,24},{24,28},{1,5},{5,9},{9,... | collective-permute-start | bytes 49160 | tf_op jit(solution)/shard_map/ppermute | solution.py:14
  58.9 5.5 %collective-permute-start.5 = (bf16[4,1,8,8,32]{4,3,2,0,1:T(8,128)(2,1)S(1)}, bf16[4,1,8,8,32]{4,3,2,0,1:T(8,128)(2,1)S(1)}, u32[]{:S(2)}, u32[]{:S(2)}) collective-permute-start(bf16[4,1,8,8,32]{4,3,2,0,1:T(8,128)(2,1)S(1)} %fusion.23), channel_id=1, source_target_pairs={{4,0},{8,4},{12,8},{16,12},{20,16},{24,20},{28,24},{5,1},{9,5},{13... | collective-permute-start | bytes 49160 | tf_op jit(solution)/shard_map/ppermute | solution.py:15
  60.9 58.6 %reduce-scatter.4.cloned.1.call-start = ((), (), s32[]{:S(2)}) async-start(), calls=%async_computation.2 | async-start | bytes 81920
  65.9 0.9 copy-start.57
  66.9 0.8 copy-start.58
  67.7 0.9 copy-start.46
  68.8 0.9 copy-start.45
  69.9 0.9 copy-start.42
  69.9 1.8 copy-start.3
  71.6 188.2 %all-reduce.11.cloned.1.call-start = ((), (), s32[]{:S(2)}) async-start(), calls=%async_computation.3 | async-start | bytes 1441792 | tf_op jit(solution)/shard_map/psum | solution.py:149
  71.9 2.1 copy-start.15
  71.9 2.1 copy-start.17
  72.6 1.4 copy-start.9
  72.6 1.4 copy-start.11
  72.6 1.4 copy-start.13
  73.3 1.0 copy-start.5
  73.3 1.1 copy-start.7
  74.9 44.7 %copy-start.2 = (f32[512,64]{1,0:T(8,128)S(1)}, f32[512,64]{1,0:T(8,128)}, u32[]{:S(2)}) copy-start(f32[512,64]{1,0:T(8,128)} %copy-done.1) | copy-start | bytes 393220
  121.4 3.5 %copy-start.24 = (bf16[64,512]{1,0:T(8,128)(2,1)S(1)}, bf16[64,512]{1,0:T(8,128)(2,1)}, u32[]{:S(2)}) copy-start(bf16[64,512]{1,0:T(8,128)(2,1)} %copy-done.23) | copy-start | bytes 196612
  121.4 3.5 %copy-start.59 = (bf16[1,1,8,8,128]{4,3,2,1,0:T(8,128)(2,1)S(1)}, bf16[1,1,8,8,128]{4,3,2,1,0:T(8,128)(2,1)}, u32[]{:S(2)}) copy-start(bf16[1,1,8,8,128]{4,3,2,1,0:T(8,128)(2,1)} %reduce-scatter.4.cloned.1.call-done) | copy-start | bytes 49156
  121.5 5.7 %collective-permute-start.6 = (bf16[1,1,16,16,64]{4,3,2,1,0:T(8,128)(2,1)S(1)}, bf16[1,1,16,16,64]{4,3,2,1,0:T(8,128)(2,1)S(1)}, u32[]{:S(2)}, u32[]{:S(2)}) collective-permute-start(bf16[1,1,16,16,64]{4,3,2,1,0:T(8,128)(2,1)S(1)} %get-tuple-element.104), channel_id=1, source_target_pairs={{0,4},{4,8},{8,12},{12,16},{16,20},{20,24},{24,28},{1,5},{5,9},{9,... | collective-permute-start | bytes 98312 | tf_op jit(solution)/shard_map/ppermute | solution.py:14
  123.4 5.8 %collective-permute-start.7 = (bf16[1,1,16,16,64]{4,3,2,1,0:T(8,128)(2,1)S(1)}, bf16[1,1,16,16,64]{4,3,2,1,0:T(8,128)(2,1)S(1)}, u32[]{:S(2)}, u32[]{:S(2)}) collective-permute-start(bf16[1,1,16,16,64]{4,3,2,1,0:T(8,128)(2,1)S(1)} %get-tuple-element.105), channel_id=1, source_target_pairs={{4,0},{8,4},{12,8},{16,12},{20,16},{24,20},{28,24},{5,1},{9,5},{13... | collective-permute-start | bytes 98312 | tf_op jit(solution)/shard_map/ppermute | solution.py:15
  127.2 2.1 copy-start.53
  137.9 0.8 copy-start.50
  138.8 0.8 copy-start.51
  138.8 0.9 copy-start.49
  139.6 0.9 copy-start.19
  140.5 0.8 copy-start.48
  141.4 0.9 copy-start.27
  142.3 0.8 copy-start.54
  142.3 0.9 copy-start.56
  143.2 0.9 copy-start.26
  144.5 0.9 copy-start.25
  259.8 1.9 copy-start.52
  (7 other events, 4.7 us)
Sparse Core Ops, SparseCore 0:
  61.1 56.7 all-reduce.8
Sparse Core Ops, SparseCore 1:
  71.7 25.9 reduce-scatter.3
  127.2 132.5 all-reduce.10
where the time goes:
time: 271 us; the launch traced here: 270 us
  waiting for transfers between devices  165 us (61%)
  local copies, waits for them, and re-layouts  48.7 us (18%)
  between operations  16.6 us (6%)
  starting transfers between devices  16.1 us (6%)
  matrix products  9.78 us (4%)
  blocking collectives  8.84 us (3%)
  other arithmetic  4.97 us (2%)
    psum x1, waiting for transfers between devices, per_device(): fine_kg, down_kg = lax.psum((fine_kg, down_kg), ('gz', 'grp'))  113 us
    psum x1, waiting for transfers between devices, coarse_kernel_total(): lax.psum(partial_value.astype(jnp.bfloat16), 'gz').astype(jnp.float32)  43 us
    unnamed x156, local copies, waits for them, and re-layouts  19.7 us
    concatenate x30, local copies, waits for them, and re-layouts, convolve(): columns = jnp.concatenate(pieces, axis=-1).reshape(-1, 9 * channels)  11.2 us
    ppermute x4, starting transfers between devices, with_halo(): before = lax.ppermute(last, axis, up)  10.6 us
    all_gather x1, blocking collectives, per_device(): lax.all_gather(coarse_framed, 'grp', axis=0, tiled=True)  8.84 us
    ppermute x4, waiting for transfers between devices, with_halo(): after = lax.ppermute(initial, axis, down)  8.64 us
    dot_general x12, matrix products, convolve(): partial_value = jnp.dot(columns, rows, preferred_element_type=jnp.float32)  5.59 us
  transfers between devices with their start and end apart: 11, of which 5 were waited for; matrix products, arithmetic and copies ran while one was open for 11% of the time, Pallas kernels for 0%

commit v1 on v0

--- a/solution.py
+++ b/solution.py
@@ -103,7 +103,9 @@
 
 
 def coarse_kernel_total(partial_value):
-    return lax.psum(partial_value.astype(jnp.bfloat16), "gz").astype(jnp.float32)
+    return jnp.sum(lax.all_gather(partial_value.astype(jnp.bfloat16), "gz"), axis=0).astype(
+        jnp.float32
+    )
 
 
 def per_device(volumes, cotangent, fine_kernel, down_kernel, coarse_kernel):

time: 271 us -> 252 us (0.930)
  waiting for transfers between devices: 165 us -> 135 us
  local copies, waits for them, and re-layouts: 48.7 us -> 54.5 us
  other arithmetic: 4.97 us -> 8.85 us
    psum x1 -> x0, waiting for transfers between devices: 43 us -> none  [coarse_kernel_total(): lax.psum(partial_value.astype(jnp.bfloat16), 'gz').astype(jnp.float32)]
    unnamed x4, waiting for transfers between devices: 0.05 us -> 19.6 us
    concatenate x30, local copies, waits for them, and re-layouts: 11.2 us -> 20.6 us  [convolve(): columns = jnp.concatenate(pieces, axis=-1).reshape(-1, 9 * channels)]
    unnamed x156 -> x128, local copies, waits for them, and re-layouts: 19.7 us -> 13.7 us
    psum x1, waiting for transfers between devices: 113 us -> 109 us  [per_device(): fine_kg, down_kg = lax.psum((fine_kg, down_kg), ('gz', 'grp'))]
  transfers between devices with their start and end apart: 11 -> 11, of which waited for: 5 -> 5; matrix products, arithmetic and copies ran while one was open for 11% -> 15% of each run, Pallas kernels for 0% -> 0%
where the time goes in v1:
time: 252 us; the launch traced here: 250 us
  waiting for transfers between devices  135 us (54%)
  local copies, waits for them, and re-layouts  54.5 us (22%)
  between operations  16.6 us (7%)
  starting transfers between devices  15.8 us (6%)
  matrix products  10.4 us (4%)
  other arithmetic  8.85 us (4%)
  blocking collectives  8.85 us (4%)
    psum x1, waiting for transfers between devices, per_device(): fine_kg, down_kg = lax.psum((fine_kg, down_kg), ('gz', 'grp'))  109 us
    concatenate x30, local copies, waits for them, and re-layouts, convolve(): columns = jnp.concatenate(pieces, axis=-1).reshape(-1, 9 * channels)  20.6 us
    unnamed x4, waiting for transfers between devices  19.6 us
    unnamed x128, local copies, waits for them, and re-layouts  13.7 us
    ppermute x4, starting transfers between devices, with_halo(): before = lax.ppermute(last, axis, up)  10.4 us
    all_gather x1, blocking collectives, per_device(): lax.all_gather(coarse_framed, 'grp', axis=0, tiled=True)  8.85 us
    dot_general x12, matrix products, convolve(): partial_value = jnp.dot(columns, rows, preferred_element_type=jnp.float32)  6.23 us
    ppermute x4, waiting for transfers between devices, with_halo(): after = lax.ppermute(initial, axis, down)  6.14 us
  transfers between devices with their start and end apart: 11, of which 5 were waited for; matrix products, arithmetic and copies ran while one was open for 15% of the time, Pallas kernels for 0%

profile of v1, /device:TPU:0, one launch (start us, length us, event | category | flops | bytes accessed | tf_op | source)
XLA Modules:
  0.0 250.1 jit_solution(6151217943517745373)
XLA Ops:
  8.1 1.0 reshape.491
  9.1 2.4 collective-permute-start
  11.5 1.3 collective-permute-start.1
  12.8 1.0 concatenate.148
  13.8 1.0 reshape.503
  15.5 1.3 collective-permute-done.1
  17.0 1.2 fusion.47
  18.8 0.7 copy-done.18
  19.5 1.0 fusion.29
  20.5 0.8 pad_maximum_fusion.3
  21.4 1.5 concatenate.143
  23.2 1.3 concatenate.155
  25.6 4.8 %collective-permute-start.2 = (bf16[1,1,8,8,128]{4,3,2,0,1:T(8,128)(2,1)S(1)}, bf16[1,1,8,8,128]{4,3,2,0,1:T(8,128)(2,1)S(1)}, u32[]{:S(2)}, u32[]{:S(2)}) collective-permute-start(bf16[1,1,8,8,128]{4,3,2,0,1:T(8,128)(2,1)S(1)} %fusion.9), channel_id=1, source_target_pairs={{0,4},{4,8},{8,12},{12,16},{16,20},{20,24},{24,28},{1,5},{5,9},{9,... | collective-permute-start | bytes 49160 | tf_op jit(solution)/shard_map/ppermute | solution.py:14
  30.4 1.3 collective-permute-start.3
  31.8 0.7 copy.163
  32.6 0.7 reshape.520
  35.3 8.8 %all_gather.7 = bf16[4,3,8,8,128]{4,3,2,0,1:T(8,128)(2,1)S(1)} all-gather(bf16[1,3,8,8,128]{4,3,2,0,1:T(8,128)(2,1)S(1)} %pad_maximum_fusion.5), channel_id=1, replica_groups=mesh['gz'=8,'grp'=4] {'grp'}, dimensions={0}, use_global_device_ids=true | all-gather | bytes 245760 | tf_op jit(solution)/shard_map/all_gather | solution.py:125
  46.3 0.8 reshape.500
  47.0 1.5 multiply_convert_fusion.4
  48.5 0.9 copy.197
  49.4 0.9 fusion.5
  50.5 0.9 copy.164
  51.4 1.0 fusion.26
  52.3 1.6 collective-permute-start.4
  54.0 1.3 collective-permute-start.5
  55.5 4.4 %collective-permute-done.5 = bf16[4,1,8,8,32]{4,3,2,0,1:T(8,128)(2,1)S(1)} collective-permute-done((bf16[4,1,8,8,32]{4,3,2,0,1:T(8,128)(2,1)S(1)}, bf16[4,1,8,8,32]{4,3,2,0,1:T(8,128)(2,1)S(1)}, u32[]{:S(2)}, u32[]{:S(2)}) %collective-permute-start.5) | collective-permute-done | bytes 16416 | tf_op jit(solution)/shard_map/ppermute | solution.py:15
  60.8 0.8 fusion.43
  61.6 0.7 fusion.44
  62.3 0.9 copy.167
  69.4 1.2 fusion.52
  70.6 1.1 concatenate.171
  72.0 1.1 concatenate.161
  73.0 0.8 fusion.7
  74.0 0.7 pad_maximum_fusion
  75.1 1.7 rev.7
  77.1 0.7 copy.191
  79.2 1.2 concatenate.186
  80.4 19.5 %reduce-scatter.4.cloned.1.call-done = bf16[1,1,8,8,128]{4,3,2,1,0:T(8,128)(2,1)} async-done(((bf16[4,1,8,8,128]{4,3,2,1,0:T(8,128)(2,1)}), bf16[1,1,8,8,128]{4,3,2,1,0:T(8,128)(2,1)}) %reduce-scatter.4.cloned.1.call-update) | async-done | bytes 16400
  100.0 1.0 multiply_convert_fusion
  101.4 1.5 collective-permute-start.6
  102.9 1.5 collective-permute-start.7
  104.9 0.9 fusion.40
  106.2 0.9 concatenate.187
  108.6 1.2 fusion.45
  109.7 0.7 fusion.46
  110.5 1.6 copy.184
  112.2 1.6 copy.185
  113.8 1.6 copy.186
  115.4 1.0 copy.187
  116.4 1.0 copy.188
  117.4 1.0 copy.189
  118.4 1.0 copy.190
  119.4 0.8 constant_dynamic-update-slice_fusion.43
  120.2 0.8 constant_dynamic-update-slice_fusion.42
  121.1 0.8 constant_dynamic-update-slice_fusion.41
  122.0 0.9 fusion.54
  123.0 1.0 pad_maximum_fusion.1
  123.9 1.2 concatenate.174
  126.6 0.8 convert_element_type.160
  127.3 1.8 reduce_sum.12
  129.1 0.8 convert_element_type.166
  129.9 109.3 %all-reduce.8.cloned.1.call-done = (f32[1728,64]{0,1:T(8,128)}, f32[512,128]{1,0:T(8,128)}) async-done(((f32[1728,64]{0,1:T(8,128)}, f32[512,128]{1,0:T(8,128)}), (f32[1728,64]{0,1:T(8,128)}, f32[512,128]{1,0:T(8,128)})) %all-reduce.8.cloned.1.call-update) | async-done | bytes 704528 | tf_op jit(solution)/shard_map/psum | solution.py:151
  239.2 1.8 copy.253
  241.0 1.7 copy.254
  (191 shorter events, 20.6 us)
Async XLA Ops:
  8.0 17.4 %copy-start = (bf16[512,128]{1,0:T(8,128)(2,1)S(1)}, bf16[512,128]{1,0:T(8,128)(2,1)}, u32[]{:S(2)}) copy-start(bf16[512,128]{1,0:T(8,128)(2,1)} %param.8) | copy-start | bytes 393220
  8.0 92.0 %reduce-scatter.4.cloned.1.call-start = ((), (), s32[]{:S(2)}) async-start(), calls=%async_computation.2 | async-start | bytes 81920
  9.1 6.4 %collective-permute-start = (bf16[1,1,16,16,64]{4,3,2,1,0:T(8,128)(2,1)S(1)}, bf16[1,1,16,16,64]{4,3,2,1,0:T(8,128)(2,1)S(1)}, u32[]{:S(2)}, u32[]{:S(2)}) collective-permute-start(bf16[1,1,16,16,64]{4,3,2,1,0:T(8,128)(2,1)S(1)} %get-tuple-element.108), channel_id=1, source_target_pairs={{0,4},{4,8},{8,12},{12,16},{16,20},{20,24},{24,28},{1,5},{5,9},{9,... | collective-permute-start | bytes 98312 | tf_op jit(solution)/shard_map/ppermute | solution.py:14
  11.5 5.3 %collective-permute-start.1 = (bf16[1,1,16,16,64]{4,3,2,1,0:T(8,128)(2,1)S(1)}, bf16[1,1,16,16,64]{4,3,2,1,0:T(8,128)(2,1)S(1)}, u32[]{:S(2)}, u32[]{:S(2)}) collective-permute-start(bf16[1,1,16,16,64]{4,3,2,1,0:T(8,128)(2,1)S(1)} %get-tuple-element.109), channel_id=1, source_target_pairs={{4,0},{8,4},{12,8},{16,12},{20,16},{24,20},{28,24},{5,1},{9,5},{13... | collective-permute-start | bytes 98312 | tf_op jit(solution)/shard_map/ppermute | solution.py:15
  18.2 3.0 %copy-start.3 = (bf16[1,2,16,16,64]{4,3,2,1,0:T(8,128)(2,1)}, bf16[1,2,16,16,64]{4,3,2,1,0:T(8,128)(2,1)S(1)}, u32[]{:S(2)}) copy-start(bf16[1,2,16,16,64]{4,3,2,1,0:T(8,128)(2,1)S(1)} %get-tuple-element.77) | copy-start | bytes 196612
  18.2 3.0 %copy-start.5 = (bf16[1,2,16,16,64]{4,3,2,1,0:T(8,128)(2,1)}, bf16[1,2,16,16,64]{4,3,2,1,0:T(8,128)(2,1)S(1)}, u32[]{:S(2)}) copy-start(bf16[1,2,16,16,64]{4,3,2,1,0:T(8,128)(2,1)S(1)} %get-tuple-element.78) | copy-start | bytes 196612
  18.3 3.0 %copy-start.7 = (bf16[1,2,16,16,64]{4,3,2,1,0:T(8,128)(2,1)}, bf16[1,2,16,16,64]{4,3,2,1,0:T(8,128)(2,1)S(1)}, u32[]{:S(2)}) copy-start(bf16[1,2,16,16,64]{4,3,2,1,0:T(8,128)(2,1)S(1)} %get-tuple-element.79) | copy-start | bytes 196612
  18.3 3.0 %copy-start.9 = (bf16[1,2,16,16,64]{4,3,2,1,0:T(8,128)(2,1)}, bf16[1,2,16,16,64]{4,3,2,1,0:T(8,128)(2,1)S(1)}, u32[]{:S(2)}) copy-start(bf16[1,2,16,16,64]{4,3,2,1,0:T(8,128)(2,1)S(1)} %get-tuple-element.80) | copy-start | bytes 196612
  18.3 3.0 %copy-start.11 = (bf16[1,2,16,16,64]{4,3,2,1,0:T(8,128)(2,1)}, bf16[1,2,16,16,64]{4,3,2,1,0:T(8,128)(2,1)S(1)}, u32[]{:S(2)}) copy-start(bf16[1,2,16,16,64]{4,3,2,1,0:T(8,128)(2,1)S(1)} %get-tuple-element.81) | copy-start | bytes 196612
  18.3 3.0 %copy-start.13 = (bf16[1,2,16,16,64]{4,3,2,1,0:T(8,128)(2,1)}, bf16[1,2,16,16,64]{4,3,2,1,0:T(8,128)(2,1)S(1)}, u32[]{:S(2)}) copy-start(bf16[1,2,16,16,64]{4,3,2,1,0:T(8,128)(2,1)S(1)} %get-tuple-element.82) | copy-start | bytes 196612
  18.3 6.3 %copy-start.15 = (bf16[1,2,16,16,64]{4,3,2,1,0:T(8,128)(2,1)}, bf16[1,2,16,16,64]{4,3,2,1,0:T(8,128)(2,1)S(1)}, u32[]{:S(2)}) copy-start(bf16[1,2,16,16,64]{4,3,2,1,0:T(8,128)(2,1)S(1)} %get-tuple-element.83) | copy-start | bytes 196612
  18.3 1.2 copy-start.18
  21.3 1.5 copy-start.33
  21.3 1.9 copy-start.26
  21.3 1.9 copy-start.27
  21.3 1.9 copy-start.28
  21.3 1.9 copy-start.29
  21.4 1.9 copy-start.30
  24.5 7.3 %copy-start.36 = (bf16[4,1,64,32]{2,3,1,0:T(8,128)(2,1)S(1)}, bf16[4,1,64,32]{2,3,1,0:T(8,128)(2,1)}, u32[]{:S(2)}) copy-start(bf16[4,1,64,32]{2,3,1,0:T(8,128)(2,1)} %param.6) | copy-start | bytes 49156
  24.9 10.4 %copy-start.16 = (f32[512,64]{0,1:T(8,128)}, f32[512,64]{0,1:T(8,128)S(1)}, u32[]{:S(2)}) copy-start(f32[512,64]{0,1:T(8,128)S(1)} %convolution_add_fusion.2) | copy-start | bytes 393220
  25.0 19.2 %copy-start.1 = (f32[512,64]{1,0:T(8,128)}, f32[512,64]{1,0:T(8,128)S(1)}, u32[]{:S(2)}) copy-start(f32[512,64]{1,0:T(8,128)S(1)} %copy.154) | copy-start | bytes 393220
  25.4 9.9 %copy-start.21 = (bf16[64,512]{1,0:T(8,128)(2,1)}, bf16[64,512]{1,0:T(8,128)(2,1)S(1)}, u32[]{:S(2)}) copy-start(bf16[64,512]{1,0:T(8,128)(2,1)S(1)} %reshape.495) | copy-start | bytes 196612
  25.6 9.7 %collective-permute-start.2 = (bf16[1,1,8,8,128]{4,3,2,0,1:T(8,128)(2,1)S(1)}, bf16[1,1,8,8,128]{4,3,2,0,1:T(8,128)(2,1)S(1)}, u32[]{:S(2)}, u32[]{:S(2)}) collective-permute-start(bf16[1,1,8,8,128]{4,3,2,0,1:T(8,128)(2,1)S(1)} %fusion.9), channel_id=1, source_target_pairs={{0,4},{4,8},{8,12},{12,16},{16,20},{20,24},{24,28},{1,5},{5,9},{9,... | collective-permute-start | bytes 49160 | tf_op jit(solution)/shard_map/ppermute | solution.py:14
  30.4 4.8 %collective-permute-start.3 = (bf16[1,1,8,8,128]{4,3,2,0,1:T(8,128)(2,1)S(1)}, bf16[1,1,8,8,128]{4,3,2,0,1:T(8,128)(2,1)S(1)}, u32[]{:S(2)}, u32[]{:S(2)}) collective-permute-start(bf16[1,1,8,8,128]{4,3,2,0,1:T(8,128)(2,1)S(1)} %fusion.9), channel_id=1, source_target_pairs={{4,0},{8,4},{12,8},{16,12},{20,16},{24,20},{28,24},{5,1},{9,5},{13... | collective-permute-start | bytes 49160 | tf_op jit(solution)/shard_map/ppermute | solution.py:15
  44.4 0.9 copy-start.20
  46.2 2.3 copy-start.31
  52.3 3.2 %collective-permute-start.4 = (bf16[4,1,8,8,32]{4,3,2,0,1:T(8,128)(2,1)S(1)}, bf16[4,1,8,8,32]{4,3,2,0,1:T(8,128)(2,1)S(1)}, u32[]{:S(2)}, u32[]{:S(2)}) collective-permute-start(bf16[4,1,8,8,32]{4,3,2,0,1:T(8,128)(2,1)S(1)} %fusion.26), channel_id=1, source_target_pairs={{0,4},{4,8},{8,12},{12,16},{16,20},{20,24},{24,28},{1,5},{5,9},{9,... | collective-permute-start | bytes 49160 | tf_op jit(solution)/shard_map/ppermute | solution.py:14
  54.0 6.0 %collective-permute-start.5 = (bf16[4,1,8,8,32]{4,3,2,0,1:T(8,128)(2,1)S(1)}, bf16[4,1,8,8,32]{4,3,2,0,1:T(8,128)(2,1)S(1)}, u32[]{:S(2)}, u32[]{:S(2)}) collective-permute-start(bf16[4,1,8,8,32]{4,3,2,0,1:T(8,128)(2,1)S(1)} %fusion.26), channel_id=1, source_target_pairs={{4,0},{8,4},{12,8},{16,12},{20,16},{24,20},{28,24},{5,1},{9,5},{13... | collective-permute-start | bytes 49160 | tf_op jit(solution)/shard_map/ppermute | solution.py:15
  55.5 4.4 %copy-start.40 = (bf16[4,1,8,8,32]{4,3,2,0,1:T(8,128)(2,1)}, bf16[4,1,8,8,32]{4,3,2,0,1:T(8,128)(2,1)S(1)}, u32[]{:S(2)}) copy-start(bf16[4,1,8,8,32]{4,3,2,0,1:T(8,128)(2,1)S(1)} %collective-permute-done.4) | copy-start | bytes 49156
  60.0 0.6 copy-start.41
  60.8 5.6 %copy-start.32 = (f32[256,32]{0,1:T(8,128)S(1)}, f32[256,32]{0,1:T(8,128)}, u32[]{:S(2)}) copy-start(f32[256,32]{0,1:T(8,128)} %copy-done.31) | copy-start | bytes 98308
  60.8 5.6 %copy-start.44 = (f32[256,32]{0,1:T(8,128)S(1)}, f32[256,32]{0,1:T(8,128)}, u32[]{:S(2)}) copy-start(f32[256,32]{0,1:T(8,128)} %reshape.520) | copy-start | bytes 98308
  60.8 8.6 %copy-start.39 = (bf16[1,3,3,32,128]{4,3,2,1,0:T(8,128)(2,1)S(1)}, bf16[1,3,3,32,128]{4,3,2,1,0:T(8,128)(2,1)}, u32[]{:S(2)}) copy-start(bf16[1,3,3,32,128]{4,3,2,1,0:T(8,128)(2,1)} %copy.175) | copy-start | bytes 221188
  61.6 10.1 %copy-start.38 = (bf16[1,3,3,32,128]{4,3,2,1,0:T(8,128)(2,1)S(1)}, bf16[1,3,3,32,128]{4,3,2,1,0:T(8,128)(2,1)}, u32[]{:S(2)}) copy-start(bf16[1,3,3,32,128]{4,3,2,1,0:T(8,128)(2,1)} %copy.176) | copy-start | bytes 221188
  62.3 10.7 %copy-start.35 = (bf16[1,3,3,32,128]{4,3,2,1,0:T(8,128)(2,1)S(1)}, bf16[1,3,3,32,128]{4,3,2,1,0:T(8,128)(2,1)}, u32[]{:S(2)}) copy-start(bf16[1,3,3,32,128]{4,3,2,1,0:T(8,128)(2,1)} %copy.165) | copy-start | bytes 221188
  64.3 9.6 %copy-start.37 = (bf16[1,1152,32]{1,2,0:T(8,128)(2,1)S(1)}, bf16[1,1152,32]{1,2,0:T(8,128)(2,1)}, u32[]{:S(2)}) copy-start(bf16[1,1152,32]{1,2,0:T(8,128)(2,1)} %fusion.5) | copy-start | bytes 221188
  69.4 5.3 %copy-start.19 = (bf16[1728,64]{0,1:T(8,128)(2,1)S(1)}, bf16[1728,64]{0,1:T(8,128)(2,1)}, u32[]{:S(2)}) copy-start(bf16[1728,64]{0,1:T(8,128)(2,1)} %param.7) | copy-start | bytes 663556
  73.9 53.4 %all-gather.2.cloned.1.call-start = ((), (), s32[]{:S(2)}) async-start(), calls=%async_computation.1 | async-start | bytes 1990656 | tf_op jit(solution)/shard_map/all_gather | solution.py:106
  74.7 164.5 %all-reduce.8.cloned.1.call-start = ((), (), s32[]{:S(2)}) async-start(), calls=%async_computation.3 | async-start | bytes 1441792 | tf_op jit(solution)/shard_map/psum | solution.py:151
  75.1 4.1 %copy-start.4 = (bf16[1,2,16,16,64]{4,3,2,1,0:T(8,128)(2,1)S(1)}, bf16[1,2,16,16,64]{4,3,2,1,0:T(8,128)(2,1)}, u32[]{:S(2)}) copy-start(bf16[1,2,16,16,64]{4,3,2,1,0:T(8,128)(2,1)} %copy-done.3) | copy-start | bytes 196612
  75.1 4.1 %copy-start.6 = (bf16[1,2,16,16,64]{4,3,2,1,0:T(8,128)(2,1)S(1)}, bf16[1,2,16,16,64]{4,3,2,1,0:T(8,128)(2,1)}, u32[]{:S(2)}) copy-start(bf16[1,2,16,16,64]{4,3,2,1,0:T(8,128)(2,1)} %copy-done.5) | copy-start | bytes 196612
  75.1 4.1 %copy-start.8 = (bf16[1,2,16,16,64]{4,3,2,1,0:T(8,128)(2,1)S(1)}, bf16[1,2,16,16,64]{4,3,2,1,0:T(8,128)(2,1)}, u32[]{:S(2)}) copy-start(bf16[1,2,16,16,64]{4,3,2,1,0:T(8,128)(2,1)} %copy-done.7) | copy-start | bytes 196612
  75.1 4.1 %copy-start.10 = (bf16[1,2,16,16,64]{4,3,2,1,0:T(8,128)(2,1)S(1)}, bf16[1,2,16,16,64]{4,3,2,1,0:T(8,128)(2,1)}, u32[]{:S(2)}) copy-start(bf16[1,2,16,16,64]{4,3,2,1,0:T(8,128)(2,1)} %copy-done.9) | copy-start | bytes 196612
  76.9 2.3 copy-start.12
  76.9 2.3 copy-start.14
  76.9 23.1 %copy-start.2 = (f32[512,64]{1,0:T(8,128)S(1)}, f32[512,64]{1,0:T(8,128)}, u32[]{:S(2)}) copy-start(f32[512,64]{1,0:T(8,128)} %copy-done.1) | copy-start | bytes 393220
  100.9 4.0 %copy-start.22 = (bf16[64,512]{1,0:T(8,128)(2,1)S(1)}, bf16[64,512]{1,0:T(8,128)(2,1)}, u32[]{:S(2)}) copy-start(bf16[64,512]{1,0:T(8,128)(2,1)} %copy-done.21) | copy-start | bytes 196612
  101.0 4.0 %copy-start.45 = (bf16[1,1,8,8,128]{4,3,2,1,0:T(8,128)(2,1)S(1)}, bf16[1,1,8,8,128]{4,3,2,1,0:T(8,128)(2,1)}, u32[]{:S(2)}) copy-start(bf16[1,1,8,8,128]{4,3,2,1,0:T(8,128)(2,1)} %reduce-scatter.4.cloned.1.call-done) | copy-start | bytes 49156
  101.4 5.8 %collective-permute-start.6 = (bf16[1,1,16,16,64]{4,3,2,1,0:T(8,128)(2,1)S(1)}, bf16[1,1,16,16,64]{4,3,2,1,0:T(8,128)(2,1)S(1)}, u32[]{:S(2)}, u32[]{:S(2)}) collective-permute-start(bf16[1,1,16,16,64]{4,3,2,1,0:T(8,128)(2,1)S(1)} %get-tuple-element.104), channel_id=1, source_target_pairs={{0,4},{4,8},{8,12},{12,16},{16,20},{20,24},{24,28},{1,5},{5,9},{9,... | collective-permute-start | bytes 98312 | tf_op jit(solution)/shard_map/ppermute | solution.py:14
  102.9 4.7 %collective-permute-start.7 = (bf16[1,1,16,16,64]{4,3,2,1,0:T(8,128)(2,1)S(1)}, bf16[1,1,16,16,64]{4,3,2,1,0:T(8,128)(2,1)S(1)}, u32[]{:S(2)}, u32[]{:S(2)}) collective-permute-start(bf16[1,1,16,16,64]{4,3,2,1,0:T(8,128)(2,1)S(1)} %get-tuple-element.105), channel_id=1, source_target_pairs={{4,0},{8,4},{12,8},{16,12},{20,16},{24,20},{28,24},{5,1},{9,5},{13... | collective-permute-start | bytes 98312 | tf_op jit(solution)/shard_map/ppermute | solution.py:15
  107.2 0.6 copy-start.42
  107.8 0.6 copy-start.43
  109.7 12.2 %copy-start.17 = (f32[512,64]{0,1:T(8,128)S(1)}, f32[512,64]{0,1:T(8,128)}, u32[]{:S(2)}) copy-start(f32[512,64]{0,1:T(8,128)} %copy-done.16) | copy-start | bytes 393220
  110.4 11.6 %copy-start.25 = (bf16[1,3,3,64,64]{4,3,2,1,0:T(8,128)(2,1)S(1)}, bf16[1,3,3,64,64]{4,3,2,1,0:T(8,128)(2,1)}, u32[]{:S(2)}) copy-start(bf16[1,3,3,64,64]{4,3,2,1,0:T(8,128)(2,1)} %copy.191) | copy-start | bytes 221188
  122.0 3.2 %copy-start.24 = (bf16[1,3,3,64,64]{4,3,2,1,0:T(8,128)(2,1)S(1)}, bf16[1,3,3,64,64]{4,3,2,1,0:T(8,128)(2,1)}, u32[]{:S(2)}) copy-start(bf16[1,3,3,64,64]{4,3,2,1,0:T(8,128)(2,1)} %copy.180) | copy-start | bytes 221188
  123.0 2.2 copy-start.34
  125.2 0.9 copy-start.23
Sparse Core Ops, SparseCore 0:
  74.0 25.9 reduce-scatter.3
  107.3 131.8 all-reduce.7
Sparse Core Ops, SparseCore 1:
  76.6 28.2 all-gather.1
